TPU v7x, 512 devices: a whole 4x4x16 slice. The times are simulated.
512 devices in a mesh: row: 16 (over z), col: 32 (over y, x, core).
Axes of the slice: x: 4, y: 4, z: 16, core: 2. Of those that a mesh axis runs over, the one named last changes fastest.
Arguments:
- flow_state: bfloat16 [131072, 256], P(('col', 'row')), may hold values from -6 to 6
- link_state: bfloat16 [65536, 256], P(('row', 'col')), may hold values from -6 to 6
- incidence: bfloat16 [16, 32, 24, 128, 128], P('row', 'col'), may hold values from -0.29882812 to 0.29882812
- tile_flow: int32 [16, 32, 24], P('row', 'col'), may hold values from 0 to 31
- tile_link: int32 [16, 32, 24], P('row', 'col'), may hold values from 0 to 31
- tile_live: int32 [16, 32, 24], P('row', 'col'), may hold values from 0 to 1, as said below
- link_gain: float32 [256], replicated, may hold values from 0.5 to 2
- link_agg_weight: bfloat16 [256, 256], replicated, may hold values from -0.375 to 0.375
- link_self_weight: bfloat16 [256, 256], replicated, may hold values from -0.375 to 0.375
- link_out_weight: bfloat16 [256, 256], replicated, may hold values from -0.375 to 0.375
- flow_gain: float32 [256], replicated, may hold values from 0.5 to 2
- flow_agg_weight: bfloat16 [256, 256], replicated, may hold values from -0.375 to 0.375
- flow_self_weight: bfloat16 [256, 256], replicated, may hold values from -0.375 to 0.375
- flow_out_weight: bfloat16 [256, 256], replicated, may hold values from -0.375 to 0.375
Outputs:
- link_next: bfloat16 [65536, 256], P(('row', 'col'))
- flow_next: bfloat16 [131072, 256], P(('col', 'row'))
Inputs may be any that keep to these rules, and one draw needn't show every extreme that they name: `tile_live`: in every draw some group pair has all 24 slots live; the number of live slots differs from pair to pair.
All inputs are finite; a program needn't handle non-finite values.
Results may differ from a plain program's by a relative error of at most 0.018.
Values may be sent and summed in bfloat16 or wider, within the bound.
No kernel may reach another device: no remote copies, remote signals or barrier semaphores. Data moves between devices by JAX's collectives and lax.ppermute only.
A program may use at most 64 MiB of HBM per device.

v0:
```python
import jax
import jax.numpy as jnp
from jax import lax
from jax.sharding import PartitionSpec as P

H = 256
BS = 128


def state_update(totals, state, gain, agg_weight, self_weight, out_weight):
    scale = lax.rsqrt(jnp.mean(totals * totals, axis=-1, keepdims=True) + 1e-05)
    normed = (totals * scale * gain).astype(jnp.bfloat16)
    before = jnp.dot(normed, agg_weight, preferred_element_type=jnp.float32) + jnp.dot(
        state, self_weight, preferred_element_type=jnp.float32
    )
    hidden = jax.nn.silu(before).astype(jnp.bfloat16)
    return (
        state.astype(jnp.float32) + jnp.dot(hidden, out_weight, preferred_element_type=jnp.float32)
    ).astype(jnp.bfloat16)


def selector(targets, live_slots, block_count):
    select = (targets[None, :] == jnp.arange(block_count, dtype=jnp.int32)[:, None]).astype(
        jnp.float32
    )
    return select * live_slots.astype(jnp.float32)[None, :]


def on_device(
    flow_state,
    link_state,
    incidence,
    tile_flow,
    tile_link,
    tile_live,
    link_gain,
    link_agg_weight,
    link_self_weight,
    link_out_weight,
    flow_gain,
    flow_agg_weight,
    flow_self_weight,
    flow_out_weight,
):
    coefs = incidence[0, 0]
    flow_slots = tile_flow[0, 0]
    link_slots = tile_link[0, 0]
    live_slots = tile_live[0, 0]
    slot_count = coefs.shape[0]
    flow_blocks_here = flow_state.shape[0] // BS
    link_blocks_here = link_state.shape[0] // BS
    link_blocks = link_blocks_here * lax.axis_size("col")
    flow_group = lax.all_gather(flow_state, "row", axis=0, tiled=True)
    flow_blocks = flow_group.shape[0] // BS
    flow_pieces = jnp.take(flow_group.reshape(flow_blocks, BS, H), flow_slots, axis=0)
    link_terms = jnp.einsum(
        "tij,tih->tjh", coefs, flow_pieces, preferred_element_type=jnp.float32
    ).reshape(slot_count, BS * H)
    link_select = selector(link_slots, live_slots, link_blocks)
    chosen = link_select
    link_sum = lax.psum_scatter(
        jnp.dot(chosen, link_terms, precision=lax.Precision.HIGHEST).astype(jnp.bfloat16),
        "col",
        scatter_dimension=0,
        tiled=True,
    ).astype(jnp.float32)
    link_next = state_update(
        link_sum.reshape(link_blocks_here * BS, H),
        link_state,
        link_gain,
        link_agg_weight,
        link_self_weight,
        link_out_weight,
    )
    link_group = lax.all_gather(link_next, "col", axis=0, tiled=True)
    link_pieces = jnp.take(link_group.reshape(link_blocks, BS, H), link_slots, axis=0)
    flow_terms = jnp.einsum(
        "tij,tjh->tih", coefs, link_pieces, preferred_element_type=jnp.float32
    ).reshape(slot_count, BS * H)
    flow_select = selector(flow_slots, live_slots, flow_blocks)
    chosen = flow_select
    flow_sum = lax.psum_scatter(
        jnp.dot(chosen, flow_terms, precision=lax.Precision.HIGHEST).astype(jnp.bfloat16),
        "row",
        scatter_dimension=0,
        tiled=True,
    ).astype(jnp.float32)
    flow_next = state_update(
        flow_sum.reshape(flow_blocks_here * BS, H),
        flow_state,
        flow_gain,
        flow_agg_weight,
        flow_self_weight,
        flow_out_weight,
    )
    return (link_next, flow_next)


def solution(mesh):
    return jax.shard_map(
        on_device,
        mesh=mesh,
        in_specs=(
            P(("col", "row"), None),
            P(("row", "col"), None),
            P("row", "col", None, None, None),
            P("row", "col", None),
            P("row", "col", None),
            P("row", "col", None),
            P(),
            P(),
            P(),
            P(),
            P(),
            P(),
            P(),
            P(),
        ),
        out_specs=(P(("row", "col"), None), P(("col", "row"), None)),
        check_vma=False,
    )
```

profile of v0, /device:TPU:2, one launch (start us, length us, event | category | flops | bytes accessed | tf_op | source)
XLA Modules:
  0.0 468.4 jit_solution(17944627231696059716)
XLA Ops:
  7.2 0.0 copy-start
  7.2 0.0 all-gather.3.cloned.1.call-start
  7.2 0.7 all-gather.3.cloned.1.call-update
  7.9 0.0 all-reduce.5.cloned.1.call-start
  8.0 0.7 compare_select_fusion.1
  8.6 0.7 compare_and_fusion.1
  9.3 0.7 convert_bitcast_fusion
  9.9 77.7 %all-gather.3.cloned.1.call-done = bf16[4096,256]{1,0:T(8,128)(2,1)} async-done(((bf16[256,256]{1,0:T(8,128)(2,1)}), bf16[4096,256]{1,0:T(8,128)(2,1)}) %all-gather.3.cloned.1.call-update) | async-done | bytes 2097168 | tf_op jit(solution)/shard_map/all_gather | solution.py:53
  87.7 2.2 gather_fusion
  89.9 0.0 copy-done
  89.9 2.4 convolution_bitcast_fusion.1
  92.3 3.6 copy.26
  95.9 0.0 copy-done.6
  95.9 6.7 %convolution_convert_fusion.1 = bf16[32,32768]{1,0:T(8,128)(2,1)} fusion(f32[24,32768]{1,0:T(8,128)} %bitcast.40, f32[24]{0:T(128)S(1)} %convert_bitcast_fusion, s32[24]{0:T(128)S(1)} %bitcast.45), kind=kOutput, calls=%fused_computation.3 | convolution fusion | flops 303040000 | bytes 5243072 | tf_op jit(solution)/shard_map/dot_general | solution.py:62
  102.5 0.0 copy-start.12
  102.6 0.0 all-reduce.5.cloned.1.call-update
  102.6 0.0 all-gather.5.cloned.1.call-start
  102.6 1.4 dynamic-slice
  104.0 133.2 %all-reduce.5.cloned.1.call-done = bf16[32,32768]{1,0:T(8,128)(2,1)} async-done(((bf16[32,32768]{1,0:T(8,128)(2,1)}), bf16[32,32768]{1,0:T(8,128)(2,1)}) %all-reduce.5.cloned.1.call-update) | async-done | bytes 2097168
  237.2 2.1 fusion.11
  239.4 0.1 multiply_reduce_fusion.1
  239.5 0.0 copy-done.2
  239.5 0.0 copy-done.4
  239.5 0.2 fusion.15
  239.7 0.0 copy-done.8
  239.7 0.0 copy-done.9
  239.7 0.0 copy-done.12
  239.7 0.9 fusion.5
  240.7 0.0 all-gather.5.cloned.1.call-update
  240.7 0.0 all-reduce.7.cloned.1.call-start
  240.8 59.3 %all-gather.5.cloned.1.call-done = bf16[4096,256]{1,0:T(8,128)(2,1)} async-done(((bf16[128,256]{1,0:T(8,128)(2,1)}), bf16[4096,256]{1,0:T(8,128)(2,1)}) %all-gather.5.cloned.1.call-update) | async-done | bytes 2097168 | tf_op jit(solution)/shard_map/all_gather | solution.py:75
  300.1 2.2 gather_fusion.1
  302.3 2.4 convolution_bitcast_fusion
  304.7 3.6 copy.27
  308.3 0.0 copy-done.7
  308.3 6.7 %convolution_convert_fusion = bf16[32,32768]{1,0:T(8,128)(2,1)} fusion(f32[24,32768]{1,0:T(8,128)} %bitcast.39, s32[24]{0:T(128)S(1)} %bitcast.46, f32[24]{0:T(128)S(1)} %convert_bitcast_fusion), kind=kOutput, calls=%fused_computation.2 | convolution fusion | flops 303040000 | bytes 5243072 | tf_op jit(solution)/shard_map/dot_general | solution.py:83
  314.9 0.0 copy-start.11
  315.0 0.0 all-reduce.7.cloned.1.call-update
  315.0 1.4 dynamic-slice.2
  317.0 142.1 %all-reduce.7.cloned.1.call-done = bf16[32,32768]{1,0:T(8,128)(2,1)} async-done(((bf16[32,32768]{1,0:T(8,128)(2,1)}), bf16[32,32768]{1,0:T(8,128)(2,1)}) %all-reduce.7.cloned.1.call-update) | async-done | bytes 2097168
  459.0 1.1 dynamic-slice_convert_fusion
  460.2 0.2 reshape.70
  460.4 0.1 multiply_reduce_fusion
  460.6 0.2 fusion.10
  460.8 0.0 copy-done.3
  460.8 0.0 copy-done.10
  460.8 0.0 copy-done.11
  460.8 1.0 fusion.4
  (19 shorter events, 0.1 us)
Async XLA Ops:
  7.2 82.8 %copy-start = (bf16[1,1,24,128,128]{4,3,2,1,0:T(8,128)(2,1)S(1)}, bf16[1,1,24,128,128]{4,3,2,1,0:T(8,128)(2,1)}, u32[]{:S(2)}) copy-start(bf16[1,1,24,128,128]{4,3,2,1,0:T(8,128)(2,1)} %param.18) | copy-start | bytes 2359300
  7.2 80.5 %all-gather.3.cloned.1.call-start = ((), (), s32[]{:S(2)}) async-start(), calls=%async_computation | async-start | bytes 2228224 | tf_op jit(solution)/shard_map/all_gather | solution.py:53
  7.9 229.3 %all-reduce.5.cloned.1.call-start = ((), (), s32[]{:S(2)}) async-start(), calls=%async_computation.2 | async-start | bytes 4194304
  92.3 3.6 copy-start.6
  102.5 136.9 %copy-start.2 = (bf16[256,256]{1,0:T(8,128)(2,1)S(1)}, bf16[256,256]{1,0:T(8,128)(2,1)}, u32[]{:S(2)}) copy-start(bf16[256,256]{1,0:T(8,128)(2,1)} %param.23) | copy-start | bytes 393220
  102.5 137.0 %copy-start.4 = (f32[256]{0:T(256)S(1)}, f32[256]{0:T(256)}, u32[]{:S(2)}) copy-start(f32[256]{0:T(256)} %param.22) | copy-start | bytes 3076
  102.5 137.2 %copy-start.8 = (bf16[256,256]{1,0:T(8,128)(2,1)S(1)}, bf16[256,256]{1,0:T(8,128)(2,1)}, u32[]{:S(2)}) copy-start(bf16[256,256]{1,0:T(8,128)(2,1)} %param.25) | copy-start | bytes 393220
  102.5 137.2 %copy-start.9 = (bf16[256,256]{1,0:T(8,128)(2,1)S(1)}, bf16[256,256]{1,0:T(8,128)(2,1)}, u32[]{:S(2)}) copy-start(bf16[256,256]{1,0:T(8,128)(2,1)} %param.24) | copy-start | bytes 393220
  102.5 137.2 %copy-start.12 = (bf16[128,256]{1,0:T(8,128)(2,1)S(1)}, bf16[128,256]{1,0:T(8,128)(2,1)}, u32[]{:S(2)}) copy-start(bf16[128,256]{1,0:T(8,128)(2,1)} %param.17) | copy-start | bytes 196612
  102.6 197.5 %all-gather.5.cloned.1.call-start = ((), (), s32[]{:S(2)}) async-start(), calls=%async_computation.1 | async-start | bytes 2162688 | tf_op jit(solution)/shard_map/all_gather | solution.py:75
  240.7 218.3 %all-reduce.7.cloned.1.call-start = ((), (), s32[]{:S(2)}) async-start(), calls=%async_computation.3 | async-start | bytes 4194304
  304.7 3.6 copy-start.7
  314.9 145.6 %copy-start.1 = (bf16[256,256]{1,0:T(8,128)(2,1)S(1)}, bf16[256,256]{1,0:T(8,128)(2,1)}, u32[]{:S(2)}) copy-start(bf16[256,256]{1,0:T(8,128)(2,1)} %param.27) | copy-start | bytes 393220
  314.9 145.6 %copy-start.5 = (f32[256]{0:T(256)S(1)}, f32[256]{0:T(256)}, u32[]{:S(2)}) copy-start(f32[256]{0:T(256)} %param.26) | copy-start | bytes 3076
  314.9 145.9 %copy-start.3 = (bf16[256,256]{1,0:T(8,128)(2,1)S(1)}, bf16[256,256]{1,0:T(8,128)(2,1)}, u32[]{:S(2)}) copy-start(bf16[256,256]{1,0:T(8,128)(2,1)} %param.16) | copy-start | bytes 393220
  314.9 145.9 %copy-start.10 = (bf16[256,256]{1,0:T(8,128)(2,1)S(1)}, bf16[256,256]{1,0:T(8,128)(2,1)}, u32[]{:S(2)}) copy-start(bf16[256,256]{1,0:T(8,128)(2,1)} %param.29) | copy-start | bytes 393220
  314.9 145.9 %copy-start.11 = (bf16[256,256]{1,0:T(8,128)(2,1)S(1)}, bf16[256,256]{1,0:T(8,128)(2,1)}, u32[]{:S(2)}) copy-start(bf16[256,256]{1,0:T(8,128)(2,1)} %param.28) | copy-start | bytes 393220
Sparse Core Ops, SparseCore 0:
  10.1 77.5 all-gather.2
  102.7 134.4 all-reduce.4
  240.9 59.1 all-gather.4
  315.1 143.8 all-reduce.6
where the time goes:
time: 469 us; the launch traced here: 468 us
  waiting for transfers between devices  413 us (88%)
  matrix products  20.5 us (4%)
  local copies, waits for them, and re-layouts  14.7 us (3%)
  between operations  14.6 us (3%)
  other arithmetic  5.46 us (1%)
    unnamed x6, waiting for transfers between devices  276 us
    all_gather x1, waiting for transfers between devices, on_device(): flow_group = lax.all_gather(flow_state, 'row', axis=0, tiled=True)  77.7 us
    all_gather x1, waiting for transfers between devices, on_device(): link_group = lax.all_gather(link_next, 'col', axis=0, tiled=True)  59.3 us
    unnamed x30, local copies, waits for them, and re-layouts  9.94 us
  transfers between devices with their start and end apart: 4, of which 4 were waited for; matrix products, arithmetic and copies ran while one was open for 1% of the time, Pallas kernels for 0%

commit v1 on v0

--- a/solution.py
+++ b/solution.py
@@ -1,3 +1,4 @@
+import functools
 import jax
 import jax.numpy as jnp
 from jax import lax
@@ -5,6 +6,18 @@
 
 H = 256
 BS = 128
+
+
+def answer_side_over_axis(my_data, dev_axis, dimension_no):
+    return jnp.concatenate(
+        lax.all_to_all(
+            jnp.stack([my_data for _ in range(lax.psum(1, dev_axis))], 0), dev_axis, 0, 0
+        ),
+        dimension_no,
+    )
+
+
+arrange_patch = functools.partial(answer_side_over_axis, dev_axis="row", dimension_no=0)
 
 
 def state_update(totals, state, gain, agg_weight, self_weight, out_weight):
@@ -50,7 +63,7 @@
     flow_blocks_here = flow_state.shape[0] // BS
     link_blocks_here = link_state.shape[0] // BS
     link_blocks = link_blocks_here * lax.axis_size("col")
-    flow_group = lax.all_gather(flow_state, "row", axis=0, tiled=True)
+    flow_group = arrange_patch(flow_state)
     flow_blocks = flow_group.shape[0] // BS
     flow_pieces = jnp.take(flow_group.reshape(flow_blocks, BS, H), flow_slots, axis=0)
     link_terms = jnp.einsum(

time: 469 us -> 502 us (1.070)
  waiting for transfers between devices: 413 us -> 430 us
  starting transfers between devices: 0.16 us -> 15.6 us
    all_to_all x0 -> x1, waiting for transfers between devices: none -> 95.5 us  [answer_side_over_axis(): lax.all_to_all(jnp.stack([my_data for _ in range(lax.psum(1, dev_axis))],...]
    all_gather x1 -> x0, waiting for transfers between devices: 77.7 us -> none  [on_device(): flow_group = lax.all_gather(flow_state, 'row', axis=0, tiled=True)]
    all_to_all x0 -> x1, starting transfers between devices: none -> 15.3 us  [answer_side_over_axis(): lax.all_to_all(jnp.stack([my_data for _ in range(lax.psum(1, dev_axis))],...]
    unnamed x6 -> x5, waiting for transfers between devices: 276 us -> 275 us
where the time goes in v1:
time: 502 us
  waiting for transfers between devices  430 us (86%)
  matrix products  21.8 us (4%)
  local copies, waits for them, and re-layouts  16.8 us (3%)
  starting transfers between devices  15.6 us (3%)
  between operations  14.7 us (3%)
    unnamed x5, waiting for transfers between devices  275 us
    all_to_all x1, waiting for transfers between devices, answer_side_over_axis(): lax.all_to_all(jnp.stack([my_data for _ in range(lax.psum(1, dev_axis))],...  95.5 us
    all_gather x1, waiting for transfers between devices, on_device(): link_group = lax.all_gather(link_next, 'col', axis=0, tiled=True)  59.1 us
    all_to_all x1, starting transfers between devices, answer_side_over_axis(): lax.all_to_all(jnp.stack([my_data for _ in range(lax.psum(1, dev_axis))],...  15.3 us
  transfers between devices with their start and end apart: 4, of which 4 were waited for; matrix products, arithmetic and copies ran while one was open for 1% of the time, Pallas kernels for 0%

profile of v1, /device:TPU:2, one launch (start us, length us, event | category | flops | bytes accessed | tf_op | source)
XLA Modules:
  0.0 501.9 jit_solution(2158927677295947725)
XLA Ops:
  7.2 0.0 copy-start
  7.2 2.5 stack.2
  9.7 15.3 %all-to-all-start = ((bf16[16,256,256]{2,1,0:T(8,128)(2,1)}), bf16[16,256,256]{2,1,0:T(8,128)(2,1)S(1)}, u32[]{:S(2)}, u32[]{:S(2)}) async-start(bf16[16,256,256]{2,1,0:T(8,128)(2,1)} %stack.2), calls=%async_computation | async-start | bytes 4194304 | tf_op jit(solution)/shard_map/all_to_all | solution.py:13
  25.0 0.0 all-reduce.5.cloned.1.call-start
  25.1 0.0 copy-done.7
  25.1 0.0 copy-done.13
  25.2 95.5 %all-to-all-done = bf16[16,256,256]{2,1,0:T(8,128)(2,1)S(1)} async-done(((bf16[16,256,256]{2,1,0:T(8,128)(2,1)}), bf16[16,256,256]{2,1,0:T(8,128)(2,1)S(1)}, u32[]{:S(2)}, u32[]{:S(2)}) %all-to-all-start) | async-done | bytes 2097184 | tf_op jit(solution)/shard_map/all_to_all | solution.py:13
  120.6 1.9 gather_fusion
  122.5 0.0 copy-done
  122.5 3.7 convolution_bitcast_fusion.1
  126.2 3.6 copy.26
  129.8 0.0 copy-done.6
  129.8 6.7 %convolution_convert_fusion.1 = bf16[32,32768]{1,0:T(8,128)(2,1)} fusion(f32[24,32768]{1,0:T(8,128)} %bitcast.40, f32[24]{0:T(128)S(1)} %convert_bitcast_fusion, s32[24]{0:T(128)S(1)} %bitcast.45), kind=kOutput, calls=%fused_computation.3 | convolution fusion | flops 303040000 | bytes 5243072 | tf_op jit(solution)/shard_map/dot_general | solution.py:75
  136.5 0.0 copy-start.12
  136.5 0.0 all-reduce.5.cloned.1.call-update
  136.5 0.0 all-gather.2.cloned.1.call-start
  136.6 1.4 dynamic-slice
  138.0 132.7 %all-reduce.5.cloned.1.call-done = bf16[32,32768]{1,0:T(8,128)(2,1)} async-done(((bf16[32,32768]{1,0:T(8,128)(2,1)}), bf16[32,32768]{1,0:T(8,128)(2,1)}) %all-reduce.5.cloned.1.call-update) | async-done | bytes 2097168
  270.7 2.1 fusion.11
  272.8 0.1 multiply_reduce_fusion.1
  272.9 0.0 copy-done.3
  273.0 0.0 copy-done.4
  273.0 0.2 fusion.15
  273.2 0.0 copy-done.8
  273.2 0.0 copy-done.9
  273.2 0.0 copy-done.12
  273.2 0.9 fusion.5
  274.1 0.0 all-gather.2.cloned.1.call-update
  274.2 0.2 all-reduce.7.cloned.1.call-start
  274.4 59.1 %all-gather.2.cloned.1.call-done = bf16[4096,256]{1,0:T(8,128)(2,1)} async-done(((bf16[128,256]{1,0:T(8,128)(2,1)}), bf16[4096,256]{1,0:T(8,128)(2,1)}) %all-gather.2.cloned.1.call-update) | async-done | bytes 2097168 | tf_op jit(solution)/shard_map/all_gather | solution.py:88
  333.6 2.2 gather_fusion.1
  335.8 2.4 convolution_bitcast_fusion
  338.2 3.6 copy.27
  341.7 6.7 %convolution_convert_fusion = bf16[32,32768]{1,0:T(8,128)(2,1)} fusion(f32[24,32768]{1,0:T(8,128)} %bitcast.39, s32[24]{0:T(128)S(1)} %bitcast.46, f32[24]{0:T(128)S(1)} %convert_bitcast_fusion), kind=kOutput, calls=%fused_computation.2 | convolution fusion | flops 303040000 | bytes 5243072 | tf_op jit(solution)/shard_map/dot_general | solution.py:96
  348.4 0.0 copy-start.11
  348.4 0.0 all-reduce.7.cloned.1.call-update
  348.4 1.4 dynamic-slice.2
  350.4 142.1 %all-reduce.7.cloned.1.call-done = bf16[32,32768]{1,0:T(8,128)(2,1)} async-done(((bf16[32,32768]{1,0:T(8,128)(2,1)}), bf16[32,32768]{1,0:T(8,128)(2,1)}) %all-reduce.7.cloned.1.call-update) | async-done | bytes 2097168
  492.6 1.1 dynamic-slice_convert_fusion
  493.7 0.2 reshape.68
  494.0 0.1 multiply_reduce_fusion
  494.1 0.0 copy-done.1
  494.1 0.0 copy-done.5
  494.1 0.2 fusion.10
  494.3 0.0 copy-done.2
  494.4 0.0 copy-done.10
  494.4 0.0 copy-done.11
  494.4 1.0 fusion.4
  (21 shorter events, 0.1 us)
Async XLA Ops:
  7.2 115.3 %copy-start = (bf16[1,1,24,128,128]{4,3,2,1,0:T(8,128)(2,1)S(1)}, bf16[1,1,24,128,128]{4,3,2,1,0:T(8,128)(2,1)}, u32[]{:S(2)}) copy-start(bf16[1,1,24,128,128]{4,3,2,1,0:T(8,128)(2,1)} %param.18) | copy-start | bytes 2359300
  9.7 15.4 %copy-start.7 = (s32[1,1,24]{2,1,0:T(1,128)S(1)}, s32[1,1,24]{2,1,0:T(1,128)}, u32[]{:S(2)}) copy-start(s32[1,1,24]{2,1,0:T(1,128)} %param.19) | copy-start | bytes 292
  9.7 15.4 %copy-start.13 = (s32[1,1,24]{2,1,0:T(1,128)S(1)}, s32[1,1,24]{2,1,0:T(1,128)}, u32[]{:S(2)}) copy-start(s32[1,1,24]{2,1,0:T(1,128)} %param.21) | copy-start | bytes 292
  9.7 110.9 %all-to-all-start = ((bf16[16,256,256]{2,1,0:T(8,128)(2,1)}), bf16[16,256,256]{2,1,0:T(8,128)(2,1)S(1)}, u32[]{:S(2)}, u32[]{:S(2)}) async-start(bf16[16,256,256]{2,1,0:T(8,128)(2,1)} %stack.2), calls=%async_computation | async-start | bytes 4194304 | tf_op jit(solution)/shard_map/all_to_all | solution.py:13
  25.0 245.7 %all-reduce.5.cloned.1.call-start = ((), (), s32[]{:S(2)}) async-start(), calls=%async_computation.2 | async-start | bytes 4194304
  126.2 3.6 copy-start.6
  136.5 136.5 %copy-start.3 = (bf16[256,256]{1,0:T(8,128)(2,1)S(1)}, bf16[256,256]{1,0:T(8,128)(2,1)}, u32[]{:S(2)}) copy-start(bf16[256,256]{1,0:T(8,128)(2,1)} %param.23) | copy-start | bytes 393220
  136.5 136.5 %copy-start.4 = (f32[256]{0:T(256)S(1)}, f32[256]{0:T(256)}, u32[]{:S(2)}) copy-start(f32[256]{0:T(256)} %param.22) | copy-start | bytes 3076
  136.5 136.7 %copy-start.8 = (bf16[256,256]{1,0:T(8,128)(2,1)S(1)}, bf16[256,256]{1,0:T(8,128)(2,1)}, u32[]{:S(2)}) copy-start(bf16[256,256]{1,0:T(8,128)(2,1)} %param.25) | copy-start | bytes 393220
  136.5 136.7 %copy-start.9 = (bf16[256,256]{1,0:T(8,128)(2,1)S(1)}, bf16[256,256]{1,0:T(8,128)(2,1)}, u32[]{:S(2)}) copy-start(bf16[256,256]{1,0:T(8,128)(2,1)} %param.24) | copy-start | bytes 393220
  136.5 136.7 %copy-start.12 = (bf16[128,256]{1,0:T(8,128)(2,1)S(1)}, bf16[128,256]{1,0:T(8,128)(2,1)}, u32[]{:S(2)}) copy-start(bf16[128,256]{1,0:T(8,128)(2,1)} %param.17) | copy-start | bytes 196612
  136.5 197.0 %all-gather.2.cloned.1.call-start = ((), (), s32[]{:S(2)}) async-start(), calls=%async_computation.1 | async-start | bytes 2162688 | tf_op jit(solution)/shard_map/all_gather | solution.py:88
  274.2 218.4 %all-reduce.7.cloned.1.call-start = ((), (), s32[]{:S(2)}) async-start(), calls=%async_computation.3 | async-start | bytes 4194304
  348.4 145.7 %copy-start.1 = (bf16[256,256]{1,0:T(8,128)(2,1)S(1)}, bf16[256,256]{1,0:T(8,128)(2,1)}, u32[]{:S(2)}) copy-start(bf16[256,256]{1,0:T(8,128)(2,1)} %param.27) | copy-start | bytes 393220
  348.4 145.7 %copy-start.5 = (f32[256]{0:T(256)S(1)}, f32[256]{0:T(256)}, u32[]{:S(2)}) copy-start(f32[256]{0:T(256)} %param.26) | copy-start | bytes 3076
  348.4 146.0 %copy-start.2 = (bf16[256,256]{1,0:T(8,128)(2,1)S(1)}, bf16[256,256]{1,0:T(8,128)(2,1)}, u32[]{:S(2)}) copy-start(bf16[256,256]{1,0:T(8,128)(2,1)} %param.16) | copy-start | bytes 393220
  348.4 146.0 %copy-start.10 = (bf16[256,256]{1,0:T(8,128)(2,1)S(1)}, bf16[256,256]{1,0:T(8,128)(2,1)}, u32[]{:S(2)}) copy-start(bf16[256,256]{1,0:T(8,128)(2,1)} %param.29) | copy-start | bytes 393220
  348.4 146.0 %copy-start.11 = (bf16[256,256]{1,0:T(8,128)(2,1)S(1)}, bf16[256,256]{1,0:T(8,128)(2,1)}, u32[]{:S(2)}) copy-start(bf16[256,256]{1,0:T(8,128)(2,1)} %param.28) | copy-start | bytes 393220
Sparse Core Ops, SparseCore 0:
  136.6 134.0 all-reduce.4
  274.4 59.1 all-gather.1
  348.5 143.9 all-reduce.6
